TPU v7x, 32 devices: a whole 2x2x4 slice. The times are simulated.
32 devices in a mesh: row: 4 (over y, x), col: 8 (over z, core).
Axes of the slice: x: 2, y: 2, z: 4, core: 2. Of those that a mesh axis runs over, the one named last changes fastest.
Arguments:
- queries: float32 [2, 192, 20480], P(None, 'col', 'row'), may hold values from -6 to 6
- precond: float32 [20480, 20480], P('row', 'col'), may hold values from -0.0390625 to 0.0390625
- column_gain: float32 [20480], P('col'), may hold values from 0.5 to 2
- store: bfloat16 [12288, 20480], P('row', 'col'), may hold values from -0.0390625 to 0.0390625
Outputs:
- scores: float32 [2, 192, 12288], P(None, 'col', 'row')
All inputs are finite; a program needn't handle non-finite values.
Results may differ from a plain program's by a relative error of at most 0.0029.
Values sent between devices are 32-bit elements; how exact they have to be, the bound alone decides.
No kernel may reach another device: no remote copies, remote signals or barrier semaphores. Data moves between devices by JAX's collectives and lax.ppermute only.
A program may use at most 128 MiB of HBM per device.

v0:
```python
import jax
import jax.numpy as jnp
from jax import lax
from jax.sharding import PartitionSpec as P


def score_block(lowered, store):
    return lax.dot_general(
        lowered, store, (((1,), (1,)), ((), ())), preferred_element_type=jnp.float32
    )


def local(queries, precond, column_gain, store):
    results = []
    for batch_index in range(queries.shape[0]):
        local_rows = queries[batch_index]
        partial_rows = jnp.dot(
            lax.all_gather(local_rows, "col", axis=0, tiled=True),
            precond,
            precision=lax.Precision.HIGHEST,
            preferred_element_type=jnp.float32,
        )
        summed = lax.psum(partial_rows, "row")
        lowered = (summed * column_gain[None, :]).astype(jnp.bfloat16)
        own_scores = lax.psum_scatter(
            score_block(lowered, store), "col", scatter_dimension=0, tiled=True
        )
        results.append(own_scores)
    return jnp.stack(results)


def solution(mesh):
    return jax.shard_map(
        local,
        mesh=mesh,
        in_specs=(P(None, "col", "row"), P("row", "col"), P("col"), P("row", "col")),
        out_specs=P(None, "col", "row"),
        check_vma=False,
    )
```

profile of v0, /device:TPU:0, one launch (start us, length us, event | category | flops | bytes accessed | tf_op | source)
XLA Modules:
  0.0 335.7 jit_solution(14430148058530714590)
XLA Ops:
  6.5 0.0 all-gather.5.cloned.1.call-start
  6.5 2.2 fusion.8
  8.7 0.0 all-gather.5.cloned.1.call-update
  8.8 0.0 all-gather.7.cloned.1.call-start
  8.8 0.7 all-gather.7.cloned.1.call-update
  9.5 0.0 all-reduce.3.cloned.1.call-start
  9.6 46.9 %all-gather.5.cloned.1.call-done = f32[1,192,5120]{2,1,0:T(8,128)} async-done(((f32[1,24,5120]{2,1,0:T(8,128)}), f32[1,192,5120]{2,1,0:T(8,128)}) %all-gather.5.cloned.1.call-update) | async-done | bytes 3932176 | tf_op jit(solution)/shard_map/all_gather | solution.py:18
  56.4 38.3 %fusion.2 = f32[192,2560]{1,0:T(8,128)} fusion(f32[5120,2560]{1,0:T(8,128)} %param.5, f32[1,192,5120]{2,1,0:T(8,128)} %all-gather.5.cloned.1.call-done), kind=kOutput, calls=%fused_computation.2 | convolution fusion | flops 30198988800 | bytes 58327040 | tf_op jit(solution)/shard_map/dot_general | solution.py:17
  94.7 7.0 %all-gather.7.cloned.1.call-done = f32[1,192,5120]{2,1,0:T(8,128)} async-done(((f32[1,24,5120]{2,1,0:T(8,128)}), f32[1,192,5120]{2,1,0:T(8,128)}) %all-gather.7.cloned.1.call-update) | async-done | bytes 3932176 | tf_op jit(solution)/shard_map/all_gather | solution.py:18
  101.7 38.3 %fusion = f32[192,2560]{1,0:T(8,128)} fusion(f32[5120,2560]{1,0:T(8,128)} %param.5, f32[1,192,5120]{2,1,0:T(8,128)} %all-gather.7.cloned.1.call-done), kind=kOutput, calls=%fused_computation | convolution fusion | flops 30198988800 | bytes 58327040 | tf_op jit(solution)/shard_map/dot_general | solution.py:17
  140.0 0.0 copy-start.1
  140.0 0.0 all-reduce.3.cloned.1.call-update
  140.0 0.0 reduce-scatter.5.cloned.1.call-start
  140.1 99.0 %all-reduce.3.cloned.1.call-done = (f32[192,2560]{1,0:T(8,128)}, f32[192,2560]{1,0:T(8,128)}) async-done(((f32[192,2560]{1,0:T(8,128)}, f32[192,2560]{1,0:T(8,128)}), (f32[192,2560]{1,0:T(8,128)}, f32[192,2560]{1,0:T(8,128)})) %all-reduce.3.cloned.1.call-update) | async-done | bytes 3932176 | tf_op jit(solution)/shard_map/psum | solution.py:23
  239.0 0.0 copy-done.1
  239.0 0.0 copy-start
  239.0 12.8 %fusion.5 = f32[192,3072]{1,0:T(8,128)} fusion(bf16[3072,2560]{1,0:T(8,128)(2,1)} %param.7, f32[192,2560]{1,0:T(8,128)} %get-tuple-element.5, f32[2560]{0:T(1024)S(1)} %copy-done.1), kind=kOutput, calls=%fused_computation.7 | convolution fusion | flops 3020881920 | bytes 20064256 | tf_op jit(solution)/shard_map/dot_general | solution.py:8
  251.9 0.0 reduce-scatter.5.cloned.1.call-update
  251.9 0.2 reduce-scatter.3.cloned.1.call-start
  252.1 0.0 copy-done
  252.2 12.1 %fusion.4 = f32[192,3072]{1,0:T(8,128)} fusion(bf16[3072,2560]{1,0:T(8,128)(2,1)} %param.7, f32[192,2560]{1,0:T(8,128)S(1)} %copy-done, f32[2560]{0:T(1024)S(1)} %copy-done.1), kind=kOutput, calls=%fused_computation.6 | convolution fusion | flops 3020881920 | bytes 20064256 | tf_op jit(solution)/shard_map/dot_general | solution.py:8
  264.3 0.0 reduce-scatter.3.cloned.1.call-update
  264.3 24.8 %reduce-scatter.5.cloned.1.call-done = f32[24,3072]{1,0:T(8,128)} async-done(((f32[192,3072]{1,0:T(8,128)}), f32[24,3072]{1,0:T(8,128)}) %reduce-scatter.5.cloned.1.call-update) | async-done | bytes 294928 | tf_op jit(solution)/shard_map/reduce_scatter | solution.py:25
  289.1 38.2 %reduce-scatter.3.cloned.1.call-done = f32[24,3072]{1,0:T(8,128)} async-done(((f32[192,3072]{1,0:T(8,128)}), f32[24,3072]{1,0:T(8,128)}) %reduce-scatter.3.cloned.1.call-update) | async-done | bytes 294928 | tf_op jit(solution)/shard_map/reduce_scatter | solution.py:25
  327.3 1.9 pad_maximum_fusion
Async XLA Ops:
  6.5 49.9 %all-gather.5.cloned.1.call-start = ((), (), s32[]{:S(2)}) async-start(), calls=%async_computation.4 | async-start | bytes 4423680 | tf_op jit(solution)/shard_map/all_gather | solution.py:18
  8.8 92.9 %all-gather.7.cloned.1.call-start = ((), (), s32[]{:S(2)}) async-start(), calls=%async_computation.5 | async-start | bytes 4423680 | tf_op jit(solution)/shard_map/all_gather | solution.py:18
  9.5 229.5 %all-reduce.3.cloned.1.call-start = ((), (), s32[]{:S(2)}) async-start(), calls=%async_computation.6 | async-start | bytes 7864320 | tf_op jit(solution)/shard_map/psum | solution.py:23
  140.0 99.1 %copy-start.1 = (f32[2560]{0:T(1024)S(1)}, f32[2560]{0:T(1024)}, u32[]{:S(2)}) copy-start(f32[2560]{0:T(1024)} %param.6) | copy-start | bytes 30724
  140.0 149.1 %reduce-scatter.5.cloned.1.call-start = ((), (), s32[]{:S(2)}) async-start(), calls=%async_computation.3 | async-start | bytes 2654208 | tf_op jit(solution)/shard_map/reduce_scatter | solution.py:25
  239.0 13.1 %copy-start = (f32[192,2560]{1,0:T(8,128)S(1)}, f32[192,2560]{1,0:T(8,128)}, u32[]{:S(2)}) copy-start(f32[192,2560]{1,0:T(8,128)} %get-tuple-element.6) | copy-start | bytes 5898244
  251.9 75.4 %reduce-scatter.3.cloned.1.call-start = ((), (), s32[]{:S(2)}) async-start(), calls=%async_computation.2 | async-start | bytes 2654208 | tf_op jit(solution)/shard_map/reduce_scatter | solution.py:25
Sparse Core Ops, SparseCore 0:
  9.0 47.4 all-gather.4
  58.1 43.5 all-gather.6
  140.1 98.8 all-reduce.2
  252.0 37.0 reduce-scatter.4
  291.3 35.9 reduce-scatter.2
where the time goes:
time: 336 us
  waiting for transfers between devices  217 us (65%)
  matrix products  102 us (30%)
  between operations  13.2 us (4%)
    psum x1, waiting for transfers between devices, local(): summed = lax.psum(partial_rows, 'row')  99 us
    dot_general x2, matrix products, local(): jnp.dot(lax.all_gather(local_rows, 'col', axis=0, tiled=True), precond, p...  76.6 us
    reduce_scatter x2, waiting for transfers between devices, local(): lax.psum_scatter(score_block(lowered, store), 'col', scatter_dimension=0,...  63 us
    all_gather x2, waiting for transfers between devices, local(): lax.all_gather(local_rows, 'col', axis=0, tiled=True)  53.8 us
    dot_general x2, matrix products, score_block(): lax.dot_general(lowered, store, (((1,), (1,)), ((), ())), preferred_eleme...  25 us
  transfers between devices with their start and end apart: 5, of which 5 were waited for; matrix products, arithmetic and copies ran while one was open for 15% of the time, Pallas kernels for 0%

commit v1 on v0

v1 whole, which is shorter than its diff:
```python
import functools

import jax
import jax.numpy as jnp
from jax import lax
from jax.experimental import pallas as pl
from jax.experimental.pallas import tpu as pltpu
from jax.sharding import PartitionSpec as P


MIB = 1024 * 1024
WHOLE = pl.BlockSpec(memory_space=pltpu.VMEM)
ALL = ("row", "col")


def split(x):
    high = x.astype(jnp.bfloat16)
    return high, (x - high.astype(jnp.float32)).astype(jnp.bfloat16)


def fitting(extent, most):
    sizes = [s for s in range(128, most + 1, 128) if extent % s == 0]
    return max(sizes) if sizes else extent


def condition_kernel(parts, priors, me_ref, *refs):
    x_refs, prior_refs, p_ref = refs[:parts], refs[parts : parts + priors], refs[parts + priors]
    out_refs, (lhs, total) = refs[parts + priors + 1 : -2], refs[-2:]
    height, tile = total.shape
    rows = height // len(out_refs)

    @pl.when(pl.program_id(0) == 0)
    def _():
        at = 0
        for x_ref in x_refs:
            n = x_ref.shape[0]
            high, low = split(x_ref[...])
            lhs[at : at + n, :] = high
            lhs[height + at : height + at + n, :] = low
            at += n

    p_high, p_low = split(p_ref[...])
    both = jnp.dot(lhs[...], p_high, preferred_element_type=jnp.float32)
    cross = jnp.dot(lhs[:height, :], p_low, preferred_element_type=jnp.float32)
    total[...] = both[:height] + (both[height:] + cross)
    columns = pl.ds(pl.multiple_of(pl.program_id(0) * tile, 128), tile)
    if len(out_refs) == 1:
        out_refs[0][:, columns] = total[...]
        return
    for slot, out_ref in enumerate(out_refs):
        group = pl.ds(pl.multiple_of((me_ref[0] ^ slot) * rows, 8), rows)
        for n, prior_ref in enumerate(prior_refs):
            out_ref[n * rows : (n + 1) * rows, columns] = prior_ref[group, columns]
        out_ref[priors * rows :, columns] = total[group, :]


def condition(me, xs, priors, precond, owners):
    height, (depth, width) = sum(x.shape[0] for x in xs), precond.shape
    rows = (1 + len(priors)) * height // owners
    tile = fitting(width, 256)
    return pl.pallas_call(
        functools.partial(condition_kernel, len(xs), len(priors)),
        out_shape=[jax.ShapeDtypeStruct((rows, width), jnp.float32)] * owners,
        grid_spec=pltpu.PrefetchScalarGridSpec(
            num_scalar_prefetch=1,
            grid=(width // tile,),
            in_specs=[WHOLE] * (len(xs) + len(priors))
            + [pl.BlockSpec((depth, tile), lambda j, me: (0, j))],
            out_specs=[WHOLE] * owners,
            scratch_shapes=[
                pltpu.VMEM((2 * height, depth), jnp.bfloat16),
                pltpu.VMEM((height, tile), jnp.float32),
            ],
        ),
        compiler_params=pltpu.CompilerParams(vmem_limit_bytes=24 * MIB),
        cost_estimate=pl.CostEstimate(
            flops=6 * height * depth * width, transcendentals=0, bytes_accessed=4 * depth * width
        ),
        name="condition",
    )(me, *xs, *priors, precond)


def score_kernel(owners, count, me_ref, *refs):
    y_refs, gain_ref, s_ref = refs[:owners], refs[owners], refs[owners + 1]
    keep_ref, send_ref, wide, lhs = refs[-4:]
    half = keep_ref.shape[0]
    height = half * 2 // count
    rows = height // owners

    @pl.when(pl.program_id(0) == 0)
    def _():
        for n in range(count):
            for slot, y_ref in enumerate(y_refs):
                group = pl.ds(pl.multiple_of((me_ref[0] ^ slot) * rows, 8), rows)
                wide[group, :] = y_ref[n * rows : (n + 1) * rows, :] * gain_ref[...]
            at = n * height // 2
            lhs[at : at + height // 2, :] = wide[: height // 2, :].astype(jnp.bfloat16)
            lhs[half + at : half + at + height // 2, :] = wide[height // 2 :, :].astype(jnp.bfloat16)

    tile = fitting(keep_ref.shape[1], 1024)
    columns = pl.ds(pl.multiple_of(pl.program_id(0) * tile, 128), tile)
    product = lax.dot_general(
        lhs[...], s_ref[columns, :], (((1,), (1,)), ((), ())), preferred_element_type=jnp.float32
    )
    keep_ref[:, columns] = product[:half]
    send_ref[:, columns] = product[half:]


def score(me, ys, count, gain, store):
    docs, depth = store.shape
    height = sum(y.shape[0] for y in ys)
    tile = fitting(docs, 1024)
    return pl.pallas_call(
        functools.partial(score_kernel, len(ys), count),
        out_shape=[jax.ShapeDtypeStruct((height // 2, docs), jnp.float32)] * 2,
        grid_spec=pltpu.PrefetchScalarGridSpec(
            num_scalar_prefetch=1,
            grid=(docs // tile,),
            in_specs=[WHOLE] * (len(ys) + 2),
            out_specs=[WHOLE] * 2,
            scratch_shapes=[
                pltpu.VMEM((height // count, depth), jnp.float32),
                pltpu.VMEM((height, depth), jnp.bfloat16),
            ],
        ),
        compiler_params=pltpu.CompilerParams(vmem_limit_bytes=12 * MIB),
        cost_estimate=pl.CostEstimate(
            flops=2 * height * depth * docs, transcendentals=0, bytes_accessed=2 * docs * depth
        ),
        name="score",
    )(me, *ys, gain, store)


def local(row_size, col_size, queries, precond, column_gain, store):
    line = col_size // 2
    me = lax.axis_index("row").astype(jnp.int32).reshape(1)

    def send(x, target):
        pairs = []
        for r in range(row_size):
            for c in range(col_size):
                to = target(r, c // 2, c % 2)
                if to is not None:
                    pairs.append((r * col_size + c, to[0] * col_size + to[1] * 2 + to[2]))
        return lax.ppermute(x, ALL, pairs)

    def to_row(x, s):
        return send(x, lambda r, z, k: (r ^ s, z, k))

    def to_line(x, s):
        return send(x, lambda r, z, k: (r, z ^ s, k))

    def swap(x):
        return send(x, lambda r, z, k: (r, z, 1 - k))

    batches, own_rows, depth = queries.shape
    own = queries.reshape(batches * own_rows, depth)
    unit = batches * own_rows

    if line == 4:
        middle = lambda r, z, k: (r, 3 - z, k) if z in (1, 2) else None
        outward = lambda r, z, k: (r, 0 if z == 1 else 3, k) if z in (1, 2) else None
        near = to_line(own, 1)
        mid_own = send(own, middle)
        mid_near = send(near, middle)
        slots = [own, near, mid_near + send(mid_own, outward), mid_own + send(mid_near, outward)]
    else:
        slots = [own] + [to_line(own, s) for s in range(1, line)]

    pair = 1 if (2 * unit) % (8 * row_size) == 0 else 2
    firsts = list(range(0, line, pair))
    batches_of = [firsts[:2]] + [[first] for first in firsts[2:]] if pair == 1 else [[f] for f in firsts]
    gain = column_gain[None, :]
    kept = {}
    scored = []
    for batch in batches_of:
        priors = []
        for first in batch:
            group = slots[first : first + pair]
            xs = group + [swap(x) for x in group]
            last = first == batch[-1]
            outs = condition(me, xs, priors if last else [], precond, row_size if last else 1)
            if not last:
                priors = priors + list(outs)
        mine = outs[0]
        for s, other in enumerate(outs[1:]):
            mine = mine + to_row(other, s + 1)
        scored.append((batch, [mine] + [to_row(mine, s) for s in range(1, row_size)]))

    for batch, ys in scored:
        keep, away = score(me, ys, len(batch), gain, store)
        back = swap(away)
        done = [first + n for first in batch for n in range(pair)]
        for n, slot in enumerate(done):
            rows = slice(n * unit, (n + 1) * unit)
            kept[slot] = keep[rows] + back[rows]
    result = kept[0]
    for s in range(1, line):
        result = result + to_line(kept[s], s)
    return result.reshape(batches, own_rows, store.shape[0])


def solution(mesh):
    row_size, col_size = mesh.shape["row"], mesh.shape["col"]

    def body(*arrays):
        return local(row_size, col_size, *arrays)

    return jax.shard_map(
        body,
        mesh=mesh,
        in_specs=(P(None, "col", "row"), P("row", "col"), P("col"), P("row", "col")),
        out_specs=P(None, "col", "row"),
        check_vma=False,
    )
```

time: 336 us -> 241 us (0.72)
  waiting for transfers between devices: 217 us -> 93 us
  matrix products: 102 us -> 0 us
  Pallas kernels: 0 us -> 99.7 us
  starting transfers between devices: 0.35 us -> 42 us
  between operations: 13.2 us -> 0.27 us
    dot_general x4 -> x0, matrix products: 102 us -> none  [the longest x2 76.6 us: local(): jnp.dot(lax.all_gather(local_rows, 'col', axis=0, tiled=True), precond, p...]
    pallas_call x0 -> x7, Pallas kernels: none -> 99.7 us  [the longest x4 83.4 us: condition(): pl.pallas_call(functools.partial(condition_kernel, len(xs), len(priors)),...]
    psum x1 -> x0, waiting for transfers between devices: 99 us -> none  [local(): summed = lax.psum(partial_rows, 'row')]
    ppermute x0 -> x33, waiting for transfers between devices: none -> 93 us  [send(): return lax.ppermute(x, ALL, pairs)]
    reduce_scatter x2 -> x0, waiting for transfers between devices: 63 us -> none  [local(): lax.psum_scatter(score_block(lowered, store), 'col', scatter_dimension=0,...]
    all_gather x2 -> x0, waiting for transfers between devices: 53.8 us -> none  [local(): lax.all_gather(local_rows, 'col', axis=0, tiled=True)]
    ppermute x0 -> x33, starting transfers between devices: none -> 42 us  [send(): return lax.ppermute(x, ALL, pairs)]
    add x0 -> x9, other arithmetic: none -> 4.41 us  [the longest x1 1.6 us: local(): mid_near + send(mid_own, outward)]
  transfers between devices with their start and end apart: 5 -> 33, of which waited for: 5 -> 10; matrix products, arithmetic and copies ran while one was open for 15% -> 2% of each run, Pallas kernels for 0% -> 42%
where the time goes in v1:
time: 241 us; the launch traced here: 240 us
  Pallas kernels  99.7 us (41%)
  waiting for transfers between devices  93 us (39%)
  starting transfers between devices  42 us (17%)
  other arithmetic  4.41 us (2%)
    ppermute x33, waiting for transfers between devices, send(): return lax.ppermute(x, ALL, pairs)  93 us
    pallas_call x4, Pallas kernels, condition(): pl.pallas_call(functools.partial(condition_kernel, len(xs), len(priors)),...  83.4 us
    ppermute x33, starting transfers between devices, send(): return lax.ppermute(x, ALL, pairs)  42 us
    pallas_call x3, Pallas kernels, score(): pl.pallas_call(functools.partial(score_kernel, len(ys), count), out_shape...  16.3 us
  transfers between devices with their start and end apart: 33, of which 10 were waited for; matrix products, arithmetic and copies ran while one was open for 2% of the time, Pallas kernels for 42%

profile of v1, /device:TPU:0, one launch (start us, length us, event | category | flops | bytes accessed | tf_op | source)
XLA Modules:
  0.0 240.2 jit_solution(17666335721710532902)
XLA Ops:
  0.0 3.1 %collective-permute-start = (f32[48,5120]{1,0:T(8,128)}, f32[48,5120]{1,0:T(8,128)S(1)}, u32[]{:S(2)}, u32[]{:S(2)}) collective-permute-start(f32[48,5120]{1,0:T(8,128)} %bitcast.5), channel_id=1, source_target_pairs={{0,2},{1,3},{2,0},{3,1},{4,6},{5,7},{6,4},{7,5},{8,10},{9,11},{10,... | collective-permute-start | bytes 2949128 | tf_op jit(solution)/shard_map/ppermute | solution.py:145
  3.1 1.6 collective-permute-start.12
  4.7 20.3 %collective-permute-done.refs_0_ = f32[48,5120]{1,0:T(8,128)S(1)} collective-permute-done((f32[48,5120]{1,0:T(8,128)}, f32[48,5120]{1,0:T(8,128)S(1)}, u32[]{:S(2)}, u32[]{:S(2)}) %collective-permute-start) | collective-permute-done | bytes 983072 | tf_op jit(solution)/shard_map/ppermute | solution.py:145
  25.0 1.6 collective-permute-start.11
  29.2 23.3 %collective-permute-done.13 = f32[48,5120]{1,0:T(8,128)} collective-permute-done((f32[48,5120]{1,0:T(8,128)}, f32[48,5120]{1,0:T(8,128)}, u32[]{:S(2)}, u32[]{:S(2)}) %collective-permute-start.13) | collective-permute-done | bytes 983072 | tf_op jit(solution)/shard_map/ppermute | solution.py:145
  52.6 1.6 add.60.refs_0_
  55.6 20.4 %condition.4.refs_2_ = f32[96,2560]{1,0:T(8,128)S(1)} custom-call(s32[1]{0:T(128)} %bitcast.me_ref, f32[48,5120]{1,0:T(8,128)S(1)} %bitcast.8, f32[48,5120]{1,0:T(8,128)S(1)} %collective-permute-done.2.refs_1_, f32[5120,2560]{1,0:T(8,128)} %refs_2_.5), custom_call_target="tpu_custom_call" | custom-call | flops 7549747200 | bytes 52428800 | tf_op jit(solution)/shard_map/condition/pallas_call | solution.py:61
  76.0 20.4 %condition.5 = (f32[48,2560]{1,0:T(8,128)S(1)}, f32[48,2560]{1,0:T(8,128)S(1)}, f32[48,2560]{1,0:T(8,128)S(1)}, f32[48,2560]{1,0:T(8,128)S(1)}) custom-call(s32[1]{0:T(128)} %bitcast.me_ref, f32[48,5120]{1,0:T(8,128)S(1)} %collective-permute-done.refs_0_, f32[48,5120]{1,0:T(8,128)S(1)} %collective-permute-done.1.refs_1_, f32[96,2560]{1,0:T(8,128)S(1)} %condition.4.refs_2_, ...), custom_call_target="tpu_custom_call" | custom-call | flops 7549747200 | bytes 52428800 | tf_op jit(solution)/shard_map/condition/pallas_call | solution.py:61
  96.4 2.5 %collective-permute-start.5 = (f32[48,2560]{1,0:T(8,128)S(1)}, f32[48,2560]{1,0:T(8,128)S(1)}, u32[]{:S(2)}, u32[]{:S(2)}) collective-permute-start(f32[48,2560]{1,0:T(8,128)S(1)} %get-tuple-element.26), channel_id=1, source_target_pairs={{0,24},{1,25},{2,26},{3,27},{4,28},{5,29},{6,30},{7,31},{8,16},{9,... | collective-permute-start | bytes 1474568 | tf_op jit(solution)/shard_map/ppermute | solution.py:145
  99.9 1.4 add.66.refs_0_
  101.4 20.4 %condition.6 = (f32[24,2560]{1,0:T(8,128)S(1)}, f32[24,2560]{1,0:T(8,128)S(1)}, f32[24,2560]{1,0:T(8,128)S(1)}, f32[24,2560]{1,0:T(8,128)S(1)}) custom-call(s32[1]{0:T(128)} %bitcast.me_ref, f32[48,5120]{1,0:T(8,128)S(1)} %add.60.refs_0_, f32[48,5120]{1,0:T(8,128)S(1)} %collective-permute-done.14.refs_1_, f32[5120,2560]{1,0:T(8,128)} %refs_2_.5), custom_call_target="tpu_custom_call" | custom-call | flops 7549747200 | bytes 52428800 | tf_op jit(solution)/shard_map/condition/pallas_call | solution.py:61
  121.8 2.5 %collective-permute-start.17 = (f32[24,2560]{1,0:T(8,128)S(1)}, f32[24,2560]{1,0:T(8,128)S(1)}, u32[]{:S(2)}, u32[]{:S(2)}) collective-permute-start(f32[24,2560]{1,0:T(8,128)S(1)} %get-tuple-element.32), channel_id=1, source_target_pairs={{0,24},{1,25},{2,26},{3,27},{4,28},{5,29},{6,30},{7,31},{8,16},{9,... | collective-permute-start | bytes 737288 | tf_op jit(solution)/shard_map/ppermute | solution.py:145
  125.5 1.5 collective-permute-start.6
  127.1 4.6 %collective-permute-done.17 = f32[24,2560]{1,0:T(8,128)S(1)} collective-permute-done((f32[24,2560]{1,0:T(8,128)S(1)}, f32[24,2560]{1,0:T(8,128)S(1)}, u32[]{:S(2)}, u32[]{:S(2)}) %collective-permute-start.17) | collective-permute-done | bytes 245792 | tf_op jit(solution)/shard_map/ppermute | solution.py:145
  131.7 1.5 collective-permute-start.7
  133.2 3.3 %collective-permute-done.16 = f32[24,2560]{1,0:T(8,128)S(1)} collective-permute-done((f32[24,2560]{1,0:T(8,128)S(1)}, f32[24,2560]{1,0:T(8,128)S(1)}, u32[]{:S(2)}, u32[]{:S(2)}) %collective-permute-start.16) | collective-permute-done | bytes 245792 | tf_op jit(solution)/shard_map/ppermute | solution.py:145
  136.5 2.4 %collective-permute-start.8 = (f32[48,2560]{1,0:T(8,128)S(1)}, f32[48,2560]{1,0:T(8,128)S(1)}, u32[]{:S(2)}, u32[]{:S(2)}) collective-permute-start(f32[48,2560]{1,0:T(8,128)S(1)} %add_add_fusion.refs_0_), channel_id=1, source_target_pairs={{0,24},{1,25},{2,26},{3,27},{4,28},{5,29},{6,30},{7,31},{8,16},{9,... | collective-permute-start | bytes 1474568 | tf_op jit(solution)/shard_map/ppermute | solution.py:145
  140.1 22.2 %condition.7 = (f32[24,2560]{1,0:T(8,128)S(1)}, f32[24,2560]{1,0:T(8,128)S(1)}, f32[24,2560]{1,0:T(8,128)S(1)}, f32[24,2560]{1,0:T(8,128)S(1)}) custom-call(s32[1]{0:T(128)} %bitcast.me_ref, f32[48,5120]{1,0:T(8,128)S(1)} %add.66.refs_0_, f32[48,5120]{1,0:T(8,128)S(1)} %collective-permute-done.24.refs_1_, f32[5120,2560]{1,0:T(8,128)} %refs_2_.5), custom_call_target="tpu_custom_call" | custom-call | flops 7549747200 | bytes 52428800 | tf_op jit(solution)/shard_map/condition/pallas_call | solution.py:61
  162.3 1.5 collective-permute-start.20
  163.8 1.5 collective-permute-start.27
  167.4 5.8 %score.3 = (f32[96,3072]{1,0:T(8,128)S(1)}, f32[96,3072]{1,0:T(8,128)S(1)}) custom-call(s32[1]{0:T(128)} %bitcast.me_ref, f32[48,2560]{1,0:T(8,128)S(1)} %add_add_fusion.refs_0_, f32[48,2560]{1,0:T(8,128)S(1)} %collective-permute-done.6.refs_1_, f32[48,2560]{1,0:T(8,128)S(1)} %collective-permute-done.7.refs_2_, ...), custom_call_target="tpu_custom_call" | custom-call | flops 3019898880 | bytes 15728640 | tf_op jit(solution)/shard_map/score/pallas_call | solution.py:113
  173.3 5.3 %score.4 = (f32[48,3072]{1,0:T(8,128)S(1)}, f32[48,3072]{1,0:T(8,128)S(1)}) custom-call(s32[1]{0:T(128)} %bitcast.me_ref, f32[24,2560]{1,0:T(8,128)S(1)} %add_add_fusion.2.refs_0_, f32[24,2560]{1,0:T(8,128)S(1)} %collective-permute-done.18.refs_1_, f32[24,2560]{1,0:T(8,128)S(1)} %collective-permute-done.19.refs_2_, ...), custom_call_target="tpu_custom_call" | custom-call | flops 1509949440 | bytes 15728640 | tf_op jit(solution)/shard_map/score/pallas_call | solution.py:113
  179.1 1.6 collective-permute-done.26
  181.2 1.5 collective-permute-start.28
  183.3 1.4 collective-permute-start.30
  184.8 4.0 %collective-permute-start.22 = (f32[48,3072]{1,0:T(8,128)S(1)}, f32[48,3072]{1,0:T(8,128)S(1)}, u32[]{:S(2)}, u32[]{:S(2)}) collective-permute-start(f32[48,3072]{1,0:T(8,128)S(1)} %add.64), channel_id=1, source_target_pairs={{0,4},{1,5},{2,6},{3,7},{4,0},{5,1},{6,2},{7,3},{8,12},{9,13},{10,... | collective-permute-start | bytes 1769480 | tf_op jit(solution)/shard_map/ppermute | solution.py:145
  190.1 5.5 %collective-permute-done.29.refs_2_ = f32[24,2560]{1,0:T(8,128)S(1)} collective-permute-done((f32[24,2560]{1,0:T(8,128)S(1)}, f32[24,2560]{1,0:T(8,128)S(1)}, u32[]{:S(2)}, u32[]{:S(2)}) %collective-permute-start.29) | collective-permute-done | bytes 245792 | tf_op jit(solution)/shard_map/ppermute | solution.py:145
  195.6 5.2 %score.5 = (f32[48,3072]{1,0:T(8,128)S(1)}, f32[48,3072]{1,0:T(8,128)S(1)}) custom-call(s32[1]{0:T(128)} %bitcast.me_ref, f32[24,2560]{1,0:T(8,128)S(1)} %add_add_fusion.1.refs_0_, f32[24,2560]{1,0:T(8,128)S(1)} %collective-permute-done.28.refs_1_, f32[24,2560]{1,0:T(8,128)S(1)} %collective-permute-done.29.refs_2_, ...), custom_call_target="tpu_custom_call" | custom-call | flops 1509949440 | bytes 15728640 | tf_op jit(solution)/shard_map/score/pallas_call | solution.py:113
  201.0 2.7 %collective-permute-start.10 = (f32[48,3072]{1,0:T(8,128)S(1)}, f32[48,3072]{1,0:T(8,128)S(1)}, u32[]{:S(2)}, u32[]{:S(2)}) collective-permute-start(f32[48,3072]{1,0:T(8,128)S(1)} %slice_add_fusion), channel_id=1, source_target_pairs={{0,2},{1,3},{2,0},{3,1},{4,6},{5,7},{6,4},{7,5},{8,10},{9,11},{10,... | collective-permute-start | bytes 1769480 | tf_op jit(solution)/shard_map/ppermute | solution.py:145
  203.8 2.8 %collective-permute-start.32 = (f32[48,3072]{1,0:T(8,128)S(1)}, f32[48,3072]{1,0:T(8,128)S(1)}, u32[]{:S(2)}, u32[]{:S(2)}) collective-permute-start(f32[48,3072]{1,0:T(8,128)S(1)} %add.70), channel_id=1, source_target_pairs={{0,6},{1,7},{2,4},{3,5},{4,2},{5,3},{6,0},{7,1},{8,14},{9,15},{10,... | collective-permute-start | bytes 1769480 | tf_op jit(solution)/shard_map/ppermute | solution.py:145
  206.6 8.3 %collective-permute-done.22 = f32[48,3072]{1,0:T(8,128)S(1)} collective-permute-done((f32[48,3072]{1,0:T(8,128)S(1)}, f32[48,3072]{1,0:T(8,128)S(1)}, u32[]{:S(2)}, u32[]{:S(2)}) %collective-permute-start.22) | collective-permute-done | bytes 589856 | tf_op jit(solution)/shard_map/ppermute | solution.py:145
  214.9 24.3 %collective-permute-done.10 = f32[48,3072]{1,0:T(8,128)S(1)} collective-permute-done((f32[48,3072]{1,0:T(8,128)S(1)}, f32[48,3072]{1,0:T(8,128)S(1)}, u32[]{:S(2)}, u32[]{:S(2)}) %collective-permute-start.10) | collective-permute-done | bytes 589856 | tf_op jit(solution)/shard_map/ppermute | solution.py:145
  (62 shorter events, 13.8 us)
Async XLA Ops:
  0.0 25.0 %collective-permute-start = (f32[48,5120]{1,0:T(8,128)}, f32[48,5120]{1,0:T(8,128)S(1)}, u32[]{:S(2)}, u32[]{:S(2)}) collective-permute-start(f32[48,5120]{1,0:T(8,128)} %bitcast.5), channel_id=1, source_target_pairs={{0,2},{1,3},{2,0},{3,1},{4,6},{5,7},{6,4},{7,5},{8,10},{9,11},{10,... | collective-permute-start | bytes 2949128 | tf_op jit(solution)/shard_map/ppermute | solution.py:145
  3.1 23.6 %collective-permute-start.12 = (f32[48,5120]{1,0:T(8,128)}, f32[48,5120]{1,0:T(8,128)}, u32[]{:S(2)}, u32[]{:S(2)}) collective-permute-start(f32[48,5120]{1,0:T(8,128)} %bitcast.6), channel_id=1, source_target_pairs={{2,4},{3,5},{4,2},{5,3},{10,12},{11,13},{12,10},{13,11},{18,20},{1... | collective-permute-start | bytes 2949128 | tf_op jit(solution)/shard_map/ppermute | solution.py:145
  25.0 4.2 %collective-permute-start.11 = (f32[48,5120]{1,0:T(8,128)S(1)}, f32[48,5120]{1,0:T(8,128)}, u32[]{:S(2)}, u32[]{:S(2)}) collective-permute-start(f32[48,5120]{1,0:T(8,128)S(1)} %collective-permute-done.refs_0_), channel_id=1, source_target_pairs={{2,4},{3,5},{4,2},{5,3},{10,12},{11,13},{12,10},{13,11},{18,20},{1... | collective-permute-start | bytes 2949128 | tf_op jit(solution)/shard_map/ppermute | solution.py:145
  26.6 25.9 %collective-permute-start.13 = (f32[48,5120]{1,0:T(8,128)}, f32[48,5120]{1,0:T(8,128)}, u32[]{:S(2)}, u32[]{:S(2)}) collective-permute-start(f32[48,5120]{1,0:T(8,128)} %collective-permute-done.12), channel_id=1, source_target_pairs={{2,0},{3,1},{4,6},{5,7},{10,8},{11,9},{12,14},{13,15},{18,16},{19,... | collective-permute-start | bytes 2949128 | tf_op jit(solution)/shard_map/ppermute | solution.py:145
  27.9 27.6 %collective-permute-start.2 = (f32[48,5120]{1,0:T(8,128)}, f32[48,5120]{1,0:T(8,128)S(1)}, u32[]{:S(2)}, u32[]{:S(2)}) collective-permute-start(f32[48,5120]{1,0:T(8,128)} %bitcast.7), channel_id=1, source_target_pairs={{0,1},{1,0},{2,3},{3,2},{4,5},{5,4},{6,7},{7,6},{8,9},{9,8},{10,11... | collective-permute-start | bytes 2949128 | tf_op jit(solution)/shard_map/ppermute | solution.py:145
  28.0 48.0 %collective-permute-start.1 = (f32[48,5120]{1,0:T(8,128)S(1)}, f32[48,5120]{1,0:T(8,128)S(1)}, u32[]{:S(2)}, u32[]{:S(2)}) collective-permute-start(f32[48,5120]{1,0:T(8,128)S(1)} %collective-permute-done.refs_0_), channel_id=1, source_target_pairs={{0,1},{1,0},{2,3},{3,2},{4,5},{5,4},{6,7},{7,6},{8,9},{9,8},{10,11... | collective-permute-start | bytes 2949128 | tf_op jit(solution)/shard_map/ppermute | solution.py:145
  54.2 47.2 %collective-permute-start.14 = (f32[48,5120]{1,0:T(8,128)S(1)}, f32[48,5120]{1,0:T(8,128)S(1)}, u32[]{:S(2)}, u32[]{:S(2)}) collective-permute-start(f32[48,5120]{1,0:T(8,128)S(1)} %add.60.refs_0_), channel_id=1, source_target_pairs={{0,1},{1,0},{2,3},{3,2},{4,5},{5,4},{6,7},{7,6},{8,9},{9,8},{10,11... | collective-permute-start | bytes 2949128 | tf_op jit(solution)/shard_map/ppermute | solution.py:145
  54.2 45.7 %collective-permute-start.23 = (f32[48,5120]{1,0:T(8,128)}, f32[48,5120]{1,0:T(8,128)S(1)}, u32[]{:S(2)}, u32[]{:S(2)}) collective-permute-start(f32[48,5120]{1,0:T(8,128)} %collective-permute-done.11), channel_id=1, source_target_pairs={{2,0},{3,1},{4,6},{5,7},{10,8},{11,9},{12,14},{13,15},{18,16},{19,... | collective-permute-start | bytes 2949128 | tf_op jit(solution)/shard_map/ppermute | solution.py:145
  96.4 27.9 %collective-permute-start.5 = (f32[48,2560]{1,0:T(8,128)S(1)}, f32[48,2560]{1,0:T(8,128)S(1)}, u32[]{:S(2)}, u32[]{:S(2)}) collective-permute-start(f32[48,2560]{1,0:T(8,128)S(1)} %get-tuple-element.26), channel_id=1, source_target_pairs={{0,24},{1,25},{2,26},{3,27},{4,28},{5,29},{6,30},{7,31},{8,16},{9,... | collective-permute-start | bytes 1474568 | tf_op jit(solution)/shard_map/ppermute | solution.py:145
  98.9 26.0 %collective-permute-start.4 = (f32[48,2560]{1,0:T(8,128)S(1)}, f32[48,2560]{1,0:T(8,128)S(1)}, u32[]{:S(2)}, u32[]{:S(2)}) collective-permute-start(f32[48,2560]{1,0:T(8,128)S(1)} %get-tuple-element.25), channel_id=1, source_target_pairs={{0,16},{1,17},{2,18},{3,19},{4,20},{5,21},{6,22},{7,23},{8,24},{9,... | collective-permute-start | bytes 1474568 | tf_op jit(solution)/shard_map/ppermute | solution.py:145
  99.4 26.0 %collective-permute-start.3 = (f32[48,2560]{1,0:T(8,128)S(1)}, f32[48,2560]{1,0:T(8,128)S(1)}, u32[]{:S(2)}, u32[]{:S(2)}) collective-permute-start(f32[48,2560]{1,0:T(8,128)S(1)} %get-tuple-element.24), channel_id=1, source_target_pairs={{0,8},{1,9},{2,10},{3,11},{4,12},{5,13},{6,14},{7,15},{8,0},{9,1},... | collective-permute-start | bytes 1474568 | tf_op jit(solution)/shard_map/ppermute | solution.py:145
  101.3 38.3 %collective-permute-start.24 = (f32[48,5120]{1,0:T(8,128)S(1)}, f32[48,5120]{1,0:T(8,128)S(1)}, u32[]{:S(2)}, u32[]{:S(2)}) collective-permute-start(f32[48,5120]{1,0:T(8,128)S(1)} %add.66.refs_0_), channel_id=1, source_target_pairs={{0,1},{1,0},{2,3},{3,2},{4,5},{5,4},{6,7},{7,6},{8,9},{9,8},{10,11... | collective-permute-start | bytes 2949128 | tf_op jit(solution)/shard_map/ppermute | solution.py:145
  121.8 9.8 %collective-permute-start.17 = (f32[24,2560]{1,0:T(8,128)S(1)}, f32[24,2560]{1,0:T(8,128)S(1)}, u32[]{:S(2)}, u32[]{:S(2)}) collective-permute-start(f32[24,2560]{1,0:T(8,128)S(1)} %get-tuple-element.32), channel_id=1, source_target_pairs={{0,24},{1,25},{2,26},{3,27},{4,28},{5,29},{6,30},{7,31},{8,16},{9,... | collective-permute-start | bytes 737288 | tf_op jit(solution)/shard_map/ppermute | solution.py:145
  124.3 12.1 %collective-permute-start.16 = (f32[24,2560]{1,0:T(8,128)S(1)}, f32[24,2560]{1,0:T(8,128)S(1)}, u32[]{:S(2)}, u32[]{:S(2)}) collective-permute-start(f32[24,2560]{1,0:T(8,128)S(1)} %get-tuple-element.31), channel_id=1, source_target_pairs={{0,16},{1,17},{2,18},{3,19},{4,20},{5,21},{6,22},{7,23},{8,24},{9,... | collective-permute-start | bytes 737288 | tf_op jit(solution)/shard_map/ppermute | solution.py:145
  124.8 14.1 %collective-permute-start.15 = (f32[24,2560]{1,0:T(8,128)S(1)}, f32[24,2560]{1,0:T(8,128)S(1)}, u32[]{:S(2)}, u32[]{:S(2)}) collective-permute-start(f32[24,2560]{1,0:T(8,128)S(1)} %get-tuple-element.30), channel_id=1, source_target_pairs={{0,8},{1,9},{2,10},{3,11},{4,12},{5,13},{6,14},{7,15},{8,0},{9,1},... | collective-permute-start | bytes 737288 | tf_op jit(solution)/shard_map/ppermute | solution.py:145
  125.5 36.8 %collective-permute-start.6 = (f32[48,2560]{1,0:T(8,128)S(1)}, f32[48,2560]{1,0:T(8,128)S(1)}, u32[]{:S(2)}, u32[]{:S(2)}) collective-permute-start(f32[48,2560]{1,0:T(8,128)S(1)} %add_add_fusion.refs_0_), channel_id=1, source_target_pairs={{0,8},{1,9},{2,10},{3,11},{4,12},{5,13},{6,14},{7,15},{8,0},{9,1},... | collective-permute-start | bytes 1474568 | tf_op jit(solution)/shard_map/ppermute | solution.py:145
  131.7 32.2 %collective-permute-start.7 = (f32[48,2560]{1,0:T(8,128)S(1)}, f32[48,2560]{1,0:T(8,128)S(1)}, u32[]{:S(2)}, u32[]{:S(2)}) collective-permute-start(f32[48,2560]{1,0:T(8,128)S(1)} %add_add_fusion.refs_0_), channel_id=1, source_target_pairs={{0,16},{1,17},{2,18},{3,19},{4,20},{5,21},{6,22},{7,23},{8,24},{9,... | collective-permute-start | bytes 1474568 | tf_op jit(solution)/shard_map/ppermute | solution.py:145
  136.5 28.9 %collective-permute-start.8 = (f32[48,2560]{1,0:T(8,128)S(1)}, f32[48,2560]{1,0:T(8,128)S(1)}, u32[]{:S(2)}, u32[]{:S(2)}) collective-permute-start(f32[48,2560]{1,0:T(8,128)S(1)} %add_add_fusion.refs_0_), channel_id=1, source_target_pairs={{0,24},{1,25},{2,26},{3,27},{4,28},{5,29},{6,30},{7,31},{8,16},{9,... | collective-permute-start | bytes 1474568 | tf_op jit(solution)/shard_map/ppermute | solution.py:145
  139.0 27.5 %collective-permute-start.18 = (f32[24,2560]{1,0:T(8,128)S(1)}, f32[24,2560]{1,0:T(8,128)S(1)}, u32[]{:S(2)}, u32[]{:S(2)}) collective-permute-start(f32[24,2560]{1,0:T(8,128)S(1)} %add_add_fusion.2.refs_0_), channel_id=1, source_target_pairs={{0,8},{1,9},{2,10},{3,11},{4,12},{5,13},{6,14},{7,15},{8,0},{9,1},... | collective-permute-start | bytes 737288 | tf_op jit(solution)/shard_map/ppermute | solution.py:145
  139.6 33.6 %collective-permute-start.19 = (f32[24,2560]{1,0:T(8,128)S(1)}, f32[24,2560]{1,0:T(8,128)S(1)}, u32[]{:S(2)}, u32[]{:S(2)}) collective-permute-start(f32[24,2560]{1,0:T(8,128)S(1)} %add_add_fusion.2.refs_0_), channel_id=1, source_target_pairs={{0,16},{1,17},{2,18},{3,19},{4,20},{5,21},{6,22},{7,23},{8,24},{9,... | collective-permute-start | bytes 737288 | tf_op jit(solution)/shard_map/ppermute | solution.py:145
  162.3 10.9 %collective-permute-start.20 = (f32[24,2560]{1,0:T(8,128)S(1)}, f32[24,2560]{1,0:T(8,128)S(1)}, u32[]{:S(2)}, u32[]{:S(2)}) collective-permute-start(f32[24,2560]{1,0:T(8,128)S(1)} %add_add_fusion.2.refs_0_), channel_id=1, source_target_pairs={{0,24},{1,25},{2,26},{3,27},{4,28},{5,29},{6,30},{7,31},{8,16},{9,... | collective-permute-start | bytes 737288 | tf_op jit(solution)/shard_map/ppermute | solution.py:145
  163.8 15.2 %collective-permute-start.27 = (f32[24,2560]{1,0:T(8,128)S(1)}, f32[24,2560]{1,0:T(8,128)S(1)}, u32[]{:S(2)}, u32[]{:S(2)}) collective-permute-start(f32[24,2560]{1,0:T(8,128)S(1)} %get-tuple-element.38), channel_id=1, source_target_pairs={{0,24},{1,25},{2,26},{3,27},{4,28},{5,29},{6,30},{7,31},{8,16},{9,... | collective-permute-start | bytes 737288 | tf_op jit(solution)/shard_map/ppermute | solution.py:145
  165.3 15.3 %collective-permute-start.26 = (f32[24,2560]{1,0:T(8,128)S(1)}, f32[24,2560]{1,0:T(8,128)S(1)}, u32[]{:S(2)}, u32[]{:S(2)}) collective-permute-start(f32[24,2560]{1,0:T(8,128)S(1)} %get-tuple-element.37), channel_id=1, source_target_pairs={{0,16},{1,17},{2,18},{3,19},{4,20},{5,21},{6,22},{7,23},{8,24},{9,... | collective-permute-start | bytes 737288 | tf_op jit(solution)/shard_map/ppermute | solution.py:145
  166.5 14.6 %collective-permute-start.25 = (f32[24,2560]{1,0:T(8,128)S(1)}, f32[24,2560]{1,0:T(8,128)S(1)}, u32[]{:S(2)}, u32[]{:S(2)}) collective-permute-start(f32[24,2560]{1,0:T(8,128)S(1)} %get-tuple-element.36), channel_id=1, source_target_pairs={{0,8},{1,9},{2,10},{3,11},{4,12},{5,13},{6,14},{7,15},{8,0},{9,1},... | collective-permute-start | bytes 737288 | tf_op jit(solution)/shard_map/ppermute | solution.py:145
  173.2 27.7 %collective-permute-start.9 = (f32[96,3072]{1,0:T(8,128)S(1)}, f32[96,3072]{1,0:T(8,128)S(1)}, u32[]{:S(2)}, u32[]{:S(2)}) collective-permute-start(f32[96,3072]{1,0:T(8,128)S(1)} %get-tuple-element.28), channel_id=1, source_target_pairs={{0,1},{1,0},{2,3},{3,2},{4,5},{5,4},{6,7},{7,6},{8,9},{9,8},{10,11... | collective-permute-start | bytes 3538952 | tf_op jit(solution)/shard_map/ppermute | solution.py:145
  178.5 6.2 %collective-permute-start.21 = (f32[48,3072]{1,0:T(8,128)S(1)}, f32[48,3072]{1,0:T(8,128)S(1)}, u32[]{:S(2)}, u32[]{:S(2)}) collective-permute-start(f32[48,3072]{1,0:T(8,128)S(1)} %get-tuple-element.34), channel_id=1, source_target_pairs={{0,1},{1,0},{2,3},{3,2},{4,5},{5,4},{6,7},{7,6},{8,9},{9,8},{10,11... | collective-permute-start | bytes 1769480 | tf_op jit(solution)/shard_map/ppermute | solution.py:145
  181.2 8.9 %collective-permute-start.28 = (f32[24,2560]{1,0:T(8,128)S(1)}, f32[24,2560]{1,0:T(8,128)S(1)}, u32[]{:S(2)}, u32[]{:S(2)}) collective-permute-start(f32[24,2560]{1,0:T(8,128)S(1)} %add_add_fusion.1.refs_0_), channel_id=1, source_target_pairs={{0,8},{1,9},{2,10},{3,11},{4,12},{5,13},{6,14},{7,15},{8,0},{9,1},... | collective-permute-start | bytes 737288 | tf_op jit(solution)/shard_map/ppermute | solution.py:145
  182.7 12.9 %collective-permute-start.29 = (f32[24,2560]{1,0:T(8,128)S(1)}, f32[24,2560]{1,0:T(8,128)S(1)}, u32[]{:S(2)}, u32[]{:S(2)}) collective-permute-start(f32[24,2560]{1,0:T(8,128)S(1)} %add_add_fusion.1.refs_0_), channel_id=1, source_target_pairs={{0,16},{1,17},{2,18},{3,19},{4,20},{5,21},{6,22},{7,23},{8,24},{9,... | collective-permute-start | bytes 737288 | tf_op jit(solution)/shard_map/ppermute | solution.py:145
  183.3 12.3 %collective-permute-start.30 = (f32[24,2560]{1,0:T(8,128)S(1)}, f32[24,2560]{1,0:T(8,128)S(1)}, u32[]{:S(2)}, u32[]{:S(2)}) collective-permute-start(f32[24,2560]{1,0:T(8,128)S(1)} %add_add_fusion.1.refs_0_), channel_id=1, source_target_pairs={{0,24},{1,25},{2,26},{3,27},{4,28},{5,29},{6,30},{7,31},{8,16},{9,... | collective-permute-start | bytes 737288 | tf_op jit(solution)/shard_map/ppermute | solution.py:145
  184.8 30.1 %collective-permute-start.22 = (f32[48,3072]{1,0:T(8,128)S(1)}, f32[48,3072]{1,0:T(8,128)S(1)}, u32[]{:S(2)}, u32[]{:S(2)}) collective-permute-start(f32[48,3072]{1,0:T(8,128)S(1)} %add.64), channel_id=1, source_target_pairs={{0,4},{1,5},{2,6},{3,7},{4,0},{5,1},{6,2},{7,3},{8,12},{9,13},{10,... | collective-permute-start | bytes 1769480 | tf_op jit(solution)/shard_map/ppermute | solution.py:145
  201.0 38.2 %collective-permute-start.10 = (f32[48,3072]{1,0:T(8,128)S(1)}, f32[48,3072]{1,0:T(8,128)S(1)}, u32[]{:S(2)}, u32[]{:S(2)}) collective-permute-start(f32[48,3072]{1,0:T(8,128)S(1)} %slice_add_fusion), channel_id=1, source_target_pairs={{0,2},{1,3},{2,0},{3,1},{4,6},{5,7},{6,4},{7,5},{8,10},{9,11},{10,... | collective-permute-start | bytes 1769480 | tf_op jit(solution)/shard_map/ppermute | solution.py:145
  203.8 35.4 %collective-permute-start.32 = (f32[48,3072]{1,0:T(8,128)S(1)}, f32[48,3072]{1,0:T(8,128)S(1)}, u32[]{:S(2)}, u32[]{:S(2)}) collective-permute-start(f32[48,3072]{1,0:T(8,128)S(1)} %add.70), channel_id=1, source_target_pairs={{0,6},{1,7},{2,4},{3,5},{4,2},{5,3},{6,0},{7,1},{8,14},{9,15},{10,... | collective-permute-start | bytes 1769480 | tf_op jit(solution)/shard_map/ppermute | solution.py:145
  (6 other events, 142.8 us)
